TPU v7x, 256 devices: a whole 4x4x8 slice. The times are simulated.
256 devices in a mesh: blk: 128 (over z, y_lo, x, core), col: 2 (over y_hi).
Axes of the slice: x: 4, y: 4 (y_hi: 2, y_lo: 2; y = y_hi * 2 + y_lo), z: 8, core: 2. Of those that a mesh axis runs over, the one named last changes fastest.
Arguments:
- tiles: bfloat16 [3072, 128, 128], P('blk'), may hold values from -0.21875 to 0.21875
- tile_rows: int32 [3072], P('blk'), may hold values from 0 to 3, as said below
- tile_cols: int32 [3072], P('blk'), may hold values from 0 to 511, as said below
- tile_count: int32 [128], P('blk'), may hold values from 3 to 24, as said below
- sketch: bfloat16 [65536, 512], P('blk', 'col'), may hold values from -6 to 6
- variant_scale: bfloat16 [65536], P('blk'), may hold values from 0.5 to 2
Outputs:
- basis_rows: float32 [65536, 512], P('blk', 'col')
Inputs may be any that keep to these rules, and one draw needn't show every extreme that they name: `tile_count`: each row group has 24, 12, 6 or 3 live slots, and at least one group has all 24 live. `tile_rows`: no two slots of a row group name the same block row and block column. Slots at or past their group's count are not part of the matrix. `tile_cols`: within one row group, all slots whose block columns lie in the same run of 4 block columns that starts at a multiple of 4 name the same block column.
All inputs are finite; a program needn't handle non-finite values.
Results may differ from a plain program's by a relative error of at most 0.0059.
Values may be sent and summed in bfloat16 or wider, within the bound.
No kernel may reach another device: no remote copies, remote signals or barrier semaphores. Data moves between devices by JAX's collectives and lax.ppermute only.
A program may use at most 128 MiB of HBM per device.

v0:
```python
import jax
import jax.numpy as jnp
from jax import lax
from jax.sharding import PartitionSpec as P

TPR = 6
RB_DEV = 4


def invert_factor(gram_matrix):
    lower_factor = jnp.linalg.cholesky(gram_matrix)
    identity = jnp.eye(gram_matrix.shape[0], dtype=jnp.float32)
    return jax.scipy.linalg.solve_triangular(lower_factor, identity, lower=True)


def gram_of(row_block):
    return lax.dot_general(
        row_block, row_block, (((0,), (0,)), ((), ())), preferred_element_type=jnp.float32
    )


def local(tiles, tile_rows, tile_cols, tile_count, sketch, variant_scale):
    sketch_width = sketch.shape[1]
    tile_edge = tiles.shape[1]
    owners = lax.axis_size("blk")
    own_blocks = sketch.shape[0] // tile_edge
    group_size = tiles.shape[0] // TPR
    own_rows = RB_DEV
    live_count = tile_count[0]
    turn_count = (live_count + group_size - 1) // group_size
    slot_ids = jnp.arange(group_size, dtype=jnp.int32)
    every_slot = jnp.arange(tiles.shape[0], dtype=jnp.int32)
    owner_ids = jnp.arange(owners, dtype=jnp.int32)
    block_ids = jnp.arange(own_blocks, dtype=jnp.int32)
    slot_owner = tile_cols // own_blocks
    slot_hits = (slot_owner[None, :] == owner_ids[:, None]) & (every_slot < live_count)[None, :]
    wanted = jnp.max(jnp.where(slot_hits, (tile_cols % own_blocks)[None, :], 0), axis=1)
    asked_blocks = lax.all_to_all(
        wanted.reshape(owners, 1), "blk", split_axis=0, concat_axis=0, tiled=True
    ).reshape(owners)

    def serve_blocks(own_panel):
        return jnp.take(
            own_panel.reshape(own_blocks, tile_edge, own_panel.shape[1]), asked_blocks, axis=0
        )

    own_scale = variant_scale.astype(jnp.float32)
    scaled_own = (own_scale[:, None] * sketch.astype(jnp.float32)).astype(jnp.bfloat16)
    fetched_sketch = lax.all_to_all(
        serve_blocks(scaled_own), "blk", split_axis=0, concat_axis=0, tiled=True
    )

    def take_group(turn_index):
        first_slot = turn_index * group_size
        tile_group = lax.dynamic_slice_in_dim(tiles, first_slot, group_size, 0)
        row_group = lax.dynamic_slice_in_dim(tile_rows, first_slot, group_size, 0)
        col_group = lax.dynamic_slice_in_dim(tile_cols, first_slot, group_size, 0)
        live_mask = (first_slot + slot_ids < live_count).astype(jnp.float32)
        return (tile_group, row_group, col_group, live_mask)

    def forward(fetched):

        def forward_step(turn_index, accumulated):
            tile_group, row_group, col_group, live_mask = take_group(turn_index)
            selected = jnp.take(fetched, col_group // own_blocks, axis=0)
            products = jnp.einsum(
                "tij,tjk->tik", tile_group, selected, preferred_element_type=jnp.float32
            )
            return accumulated.at[row_group].add(products * live_mask[:, None, None])

        start_rows = jnp.zeros((own_rows, tile_edge, sketch_width), jnp.float32)
        accumulated = lax.fori_loop(0, turn_count, forward_step, start_rows)
        return accumulated.reshape(own_rows * tile_edge, sketch_width)

    range_rows = forward(fetched_sketch).astype(jnp.bfloat16)
    row_blocks = range_rows.reshape(own_rows, tile_edge, sketch_width)

    def back_step(turn_index, accumulated):
        tile_group, row_group, col_group, live_mask = take_group(turn_index)
        selected = jnp.take(row_blocks, row_group, axis=0)
        products = jnp.einsum(
            "tji,tjk->tik", tile_group, selected, preferred_element_type=jnp.float32
        )
        return accumulated.at[col_group // own_blocks].add(products * live_mask[:, None, None])

    start_back = jnp.zeros((owners, tile_edge, sketch_width), jnp.float32)
    group_terms = lax.fori_loop(0, turn_count, back_step, start_back).astype(jnp.bfloat16)
    block_select = (asked_blocks[:, None] == block_ids[None, :]).astype(jnp.bfloat16)
    arrived_terms = lax.all_to_all(group_terms, "blk", split_axis=0, concat_axis=0, tiled=True)
    own_back = jnp.einsum(
        "qb,qik->bik", block_select, arrived_terms, preferred_element_type=jnp.float32
    )
    own_back = own_back.reshape(own_blocks * tile_edge, arrived_terms.shape[2])
    weighted_own = ((own_scale * own_scale)[:, None] * own_back).astype(jnp.bfloat16)
    fetched_weighted = lax.all_to_all(
        serve_blocks(weighted_own), "blk", split_axis=0, concat_axis=0, tiled=True
    )
    power_rows = forward(fetched_weighted).astype(jnp.bfloat16)
    total_rows = own_rows * tile_edge * lax.axis_size("blk")
    tall_rows = lax.all_to_all(power_rows, "col", split_axis=0, concat_axis=1, tiled=True)
    gram_matrix = lax.psum(gram_of(tall_rows), ("blk", "col")) / total_rows
    inverse = invert_factor(gram_matrix)
    basis_tall = jnp.dot(tall_rows.astype(jnp.float32), inverse.T, precision=lax.Precision.HIGHEST)
    basis_rows = lax.all_to_all(basis_tall, "col", split_axis=1, concat_axis=0, tiled=True)
    return basis_rows


def solution(mesh):
    placed = (P("blk", None, None), P("blk"), P("blk"), P("blk"), P("blk", "col"), P("blk"))
    return jax.shard_map(
        local, mesh=mesh, in_specs=placed, out_specs=P("blk", "col"), check_vma=False
    )
```

profile of v0, /device:TPU:1, one launch (start us, length us, event | category | flops | bytes accessed | tf_op | source)
XLA Modules:
  0.0 1198.8 jit_solution(2881214073170793643)
XLA Ops:
  8.7 14.8 %all-to-all-start = ((s32[128,1,1]{2,1,0:T(1,128)}), s32[128,1,1]{2,1,0:T(1,128)S(1)}, u32[]{:S(2)}, u32[]{:S(2)}) async-start(s32[128,1,1]{2,1,0:T(1,128)} %copy.36), calls=%async_computation | async-start | bytes 131072 | tf_op jit(solution)/shard_map/all_to_all | solution.py:38
  25.3 8.8 all-to-all-done
  36.4 6.2 gather_fusion.3
  42.6 7.4 broadcast_select_fusion
  50.1 7.2 all-to-all-start.1
  57.3 186.6 %all-to-all-done.1 = bf16[128,128,256]{2,1,0:T(8,128)(2,1)} async-done(((bf16[128,128,256]{2,1,0:T(8,128)(2,1)}), bf16[128,128,256]{2,1,0:T(8,128)(2,1)}, u32[]{:S(2)}, u32[]{:S(2)}) %all-to-all-start.1) | async-done | bytes 8388640 | tf_op jit(solution)/shard_map/all_to_all | solution.py:49
  243.9 12.0 while.41
  244.7 3.9 gather_fusion
  250.7 3.9 gather_fusion
  256.0 7.8 broadcast_in_dim.86
  263.8 8.8 while.42
  272.6 9.0 convert_element_type.70
  281.6 48.2 %all-to-all-start.2 = ((bf16[128,128,256]{2,1,0:T(8,128)(2,1)}), bf16[128,128,256]{2,1,0:T(8,128)(2,1)}, u32[]{:S(2)}, u32[]{:S(2)}) async-start(bf16[128,128,256]{2,1,0:T(8,128)(2,1)} %convert_element_type.70), calls=%async_computation.2 | async-start | bytes 16777216 | tf_op jit(solution)/shard_map/all_to_all | solution.py:89
  330.0 186.5 %all-to-all-done.2 = bf16[128,128,256]{2,1,0:T(8,128)(2,1)} async-done(((bf16[128,128,256]{2,1,0:T(8,128)(2,1)}), bf16[128,128,256]{2,1,0:T(8,128)(2,1)}, u32[]{:S(2)}, u32[]{:S(2)}) %all-to-all-start.2) | async-done | bytes 8388640 | tf_op jit(solution)/shard_map/all_to_all | solution.py:89
  516.5 7.9 fusion.29
  524.5 6.2 gather_fusion.4
  530.7 7.4 broadcast_select_fusion.1
  538.1 7.4 all-to-all-start.3
  545.6 186.6 %all-to-all-done.3 = bf16[128,128,256]{2,1,0:T(8,128)(2,1)} async-done(((bf16[128,128,256]{2,1,0:T(8,128)(2,1)}), bf16[128,128,256]{2,1,0:T(8,128)(2,1)}, u32[]{:S(2)}, u32[]{:S(2)}) %all-to-all-start.3) | async-done | bytes 8388640 | tf_op jit(solution)/shard_map/all_to_all | solution.py:95
  732.2 12.0 while.43
  744.2 9.2 all_to_all.56
  756.2 274.6 %all-reduce.3.cloned.1.call-done = f32[512,512]{0,1:T(8,128)} async-done(((f32[512,512]{0,1:T(8,128)}), f32[512,512]{0,1:T(8,128)}) %all-reduce.3.cloned.1.call-update) | async-done | bytes 1048592 | tf_op jit(solution)/shard_map/psum | solution.py:101
  1034.0 11.7 cholesky.104
  1045.9 9.8 custom-call.31
  1057.0 11.7 cholesky.217
  1068.8 10.0 custom-call.32
  1081.0 13.2 %cholesky.238 = f32[128,128]{1,0:T(8,128)} custom-call(f32[128,128]{1,0:T(8,128)} %cholesky.275), custom_call_target="Cholesky" | custom-call | tf_op jit(solution)/shard_map/jit(cholesky)/cholesky | solution.py:11
  1096.2 11.3 custom-call.33
  1108.9 11.9 cholesky.255
  1124.9 10.5 while.40
  1135.4 40.1 %custom-call.34 = f32[4,128,128]{1,2,0:T(8,128)S(1)} custom-call(f32[4,128,128]{2,1,0:T(8,128)} %get-tuple-element.368), custom_call_target="InvertDiagBlocksLowerTriangular" | custom-call | tf_op jit(solution)/shard_map/jit(_solve_triangular)/triangular_solve | solution.py:13
  1180.2 10.6 all_to_all.57
  (115 shorter events, 61.0 us)
Async XLA Ops:
  8.7 25.3 %all-to-all-start = ((s32[128,1,1]{2,1,0:T(1,128)}), s32[128,1,1]{2,1,0:T(1,128)S(1)}, u32[]{:S(2)}, u32[]{:S(2)}) async-start(s32[128,1,1]{2,1,0:T(1,128)} %copy.36), calls=%async_computation | async-start | bytes 131072 | tf_op jit(solution)/shard_map/all_to_all | solution.py:38
  50.1 193.9 %copy-start = (bf16[24,128,128]{2,1,0:T(8,128)(2,1)S(1)}, bf16[24,128,128]{2,1,0:T(8,128)(2,1)}, u32[]{:S(2)}) copy-start(bf16[24,128,128]{2,1,0:T(8,128)(2,1)} %param.16) | copy-start | bytes 2359300
  50.1 193.9 %copy-start.2 = (s32[24]{0:T(128)S(1)}, s32[24]{0:T(128)}, u32[]{:S(2)}) copy-start(s32[24]{0:T(128)} %param.18) | copy-start | bytes 292
  50.1 193.9 %copy-start.3 = (s32[24]{0:T(128)S(1)}, s32[24]{0:T(128)}, u32[]{:S(2)}) copy-start(s32[24]{0:T(128)} %param.17) | copy-start | bytes 292
  50.1 193.8 %all-to-all-start.1 = ((bf16[128,128,256]{2,1,0:T(8,128)(2,1)}), bf16[128,128,256]{2,1,0:T(8,128)(2,1)}, u32[]{:S(2)}, u32[]{:S(2)}) async-start(bf16[128,128,256]{2,1,0:T(8,128)(2,1)} %broadcast_select_fusion), calls=%async_computation.1 | async-start | bytes 16777216 | tf_op jit(solution)/shard_map/all_to_all | solution.py:49
  281.6 48.3 %copy-start.4 = (bf16[512]{0:T(512)(128)(2,1)S(1)}, bf16[512]{0:T(512)(128)(2,1)}, u32[]{:S(2)}) copy-start(bf16[512]{0:T(512)(128)(2,1)} %param.21) | copy-start | bytes 3076
  281.6 234.9 %all-to-all-start.2 = ((bf16[128,128,256]{2,1,0:T(8,128)(2,1)}), bf16[128,128,256]{2,1,0:T(8,128)(2,1)}, u32[]{:S(2)}, u32[]{:S(2)}) async-start(bf16[128,128,256]{2,1,0:T(8,128)(2,1)} %convert_element_type.70), calls=%async_computation.2 | async-start | bytes 16777216 | tf_op jit(solution)/shard_map/all_to_all | solution.py:89
  538.1 194.0 %all-to-all-start.3 = ((bf16[128,128,256]{2,1,0:T(8,128)(2,1)}), bf16[128,128,256]{2,1,0:T(8,128)(2,1)}, u32[]{:S(2)}, u32[]{:S(2)}) async-start(bf16[128,128,256]{2,1,0:T(8,128)(2,1)} %broadcast_select_fusion.1), calls=%async_computation.3 | async-start | bytes 16777216 | tf_op jit(solution)/shard_map/all_to_all | solution.py:95
  545.5 485.3 %all-reduce.3.cloned.1.call-start = ((), (), s32[]{:S(2)}) async-start(), calls=%async_computation.6 | async-start | bytes 2097152 | tf_op jit(solution)/shard_map/psum | solution.py:101
  1056.3 0.7 copy-start.1
Sparse Core Ops, SparseCore 0:
  755.0 275.8 all-reduce.2
where the time goes:
time: 1210 us; the launch traced here: 1200 us
  waiting for transfers between devices  843 us (70%)
  other arithmetic  170 us (14%)
  starting transfers between devices  77.6 us (6%)
  local copies, waits for them, and re-layouts  51.7 us (4%)
  blocking collectives  19.8 us (2%)
  matrix products  19.1 us (2%)
  between operations  17.4 us (1%)
    psum x1, waiting for transfers between devices, local(): gram_matrix = lax.psum(gram_of(tall_rows), ('blk', 'col')) / total_rows  275 us
    all_to_all x1, waiting for transfers between devices, local(): lax.all_to_all(serve_blocks(scaled_own), 'blk', split_axis=0, concat_axis...  187 us
    all_to_all x1, waiting for transfers between devices, local(): lax.all_to_all(serve_blocks(weighted_own), 'blk', split_axis=0, concat_ax...  187 us
    all_to_all x1, waiting for transfers between devices, local(): lax.all_to_all(group_terms, 'blk', split_axis=0, concat_axis=0, tiled=True)  187 us
    another operation x14, other arithmetic, invert_factor(): lower_factor = jnp.linalg.cholesky(gram_matrix)  83.2 us
    all_to_all x1, starting transfers between devices, local(): lax.all_to_all(group_terms, 'blk', split_axis=0, concat_axis=0, tiled=True)  48.2 us
    another operation x4, other arithmetic, invert_factor(): return jax.scipy.linalg.solve_triangular(lower_factor, identity, lower=True)  40.3 us
  transfers between devices with their start and end apart: 5, of which 5 were waited for; matrix products, arithmetic and copies ran while one was open for 0% of the time, Pallas kernels for 0%

commit v1 on v0

v1 whole, which is shorter than its diff:
```python
import jax
import jax.numpy as jnp
from jax import lax
from jax.experimental import pallas as pl
from jax.experimental.pallas import tpu as pltpu
from jax.sharding import PartitionSpec as P

RB_DEV = 4


def spread(rows, axes):
    return lax.all_to_all(rows, axes, split_axis=0, concat_axis=0, tiled=True)


def factor_body(gram_ref, out_ref, work_ref, row_ref):
    edge = row_ref.shape[0]
    size = gram_ref.shape[0]
    count = size // edge
    hi = lax.Precision.HIGHEST
    work_ref[...] = gram_ref[...]
    lanes = lax.broadcasted_iota(jnp.int32, (edge, edge), 1)
    rows = lax.broadcasted_iota(jnp.int32, (edge, edge), 0)

    def stage(k, _):
        base = pl.multiple_of(k * edge, edge)
        w = work_ref[pl.ds(base, edge), pl.ds(base, edge)]
        for j in range(edge):
            row = w[j:j + 1, :]
            r = lax.rsqrt(w[j:j + 1, j:j + 1])
            scaled = jnp.where(lanes[:1] == j, r, row * r)
            first = (j // 8) * 8
            low = w[first:, :]
            below = rows[first:] > j
            factor = jnp.where(below[:, :1], low[:, j:j + 1] * r, 0.0)
            kept = jnp.where(below & (lanes[first:] == j), 0.0, low)
            kept = jnp.where(rows[first:] == j, scaled, kept - factor * scaled)
            w = kept if first == 0 else jnp.concatenate([w[:first], kept], axis=0)
        inv = jnp.where(rows >= lanes, w, 0.0)
        row_ref[...] = jnp.dot(inv, work_ref[pl.ds(base, edge), :], precision=hi, preferred_element_type=jnp.float32)
        row_ref[:, pl.ds(base, edge)] = inv
        work_ref[pl.ds(base, edge), :] = row_ref[...]

        def below_block(i, _):
            at = pl.multiple_of(i * edge, edge)
            work_ref[pl.ds(at, edge), pl.ds(base, edge)] = jnp.zeros((edge, edge), jnp.float32)
            work_ref[pl.ds(at, edge), :] -= lax.dot_general(
                row_ref[:, pl.ds(at, edge)], row_ref[...], (((0,), (0,)), ((), ())),
                precision=hi, preferred_element_type=jnp.float32)
            return 0
        lax.fori_loop(k + 1, count, below_block, 0)
        return 0
    lax.fori_loop(0, count, stage, 0)
    r2 = lax.broadcasted_iota(jnp.int32, (size, size), 0)
    c2 = lax.broadcasted_iota(jnp.int32, (size, size), 1)
    out_ref[...] = jnp.where(r2 >= c2, work_ref[...], 0.0)

def invert_factor(gram):
    n = gram.shape[0]
    return pl.pallas_call(
        factor_body,
        out_shape=jax.ShapeDtypeStruct((n, n), jnp.float32),
        scratch_shapes=[pltpu.VMEM((n, n), jnp.float32), pltpu.VMEM((128, n), jnp.float32)],
    )(gram)


def local(tiles, tile_rows, tile_cols, tile_count, sketch, variant_scale):
    slots, edge, _ = tiles.shape
    width = sketch.shape[1]
    owners = lax.axis_size("blk")
    cols = lax.axis_size("col")
    own_blocks = sketch.shape[0] // edge
    blocks = owners * own_blocks
    bf16, f32 = jnp.bfloat16, jnp.float32

    own_rows = jnp.swapaxes(sketch.reshape(own_blocks, edge, width), 0, 1)
    own_scales = variant_scale.reshape(own_blocks, edge).T
    live = jnp.arange(slots, dtype=jnp.int32) < tile_count[0]
    run = jnp.where(live, tile_cols // own_blocks, -1).astype(bf16)
    member = (tile_cols % own_blocks).astype(bf16)
    notes = jnp.concatenate([run, member])
    notes = jnp.concatenate([own_scales, jnp.broadcast_to(notes, (edge, 2 * slots))], axis=1)
    notes = jnp.pad(notes, ((0, 0), (0, width - notes.shape[1])))
    packed = jnp.concatenate([own_rows, notes[:, None, :]], axis=1)
    kept = spread(packed, "blk")
    kept_rows = kept[:, :own_blocks, :].reshape(blocks, width)
    kept_notes = kept[:, own_blocks, :].astype(f32)
    kept_scale = kept_notes[:, :own_blocks].reshape(blocks, 1)
    all_runs = kept_notes[:, own_blocks : own_blocks + slots]
    all_members = kept_notes[:, own_blocks + slots : own_blocks + 2 * slots]
    all_cols = (all_runs * own_blocks + all_members).astype(jnp.int32)
    block_ids = jnp.arange(blocks, dtype=jnp.int32)
    picks = (all_cols[:, :, None] == block_ids).astype(bf16).reshape(owners * slots, blocks)

    row_ids = jnp.arange(RB_DEV, dtype=jnp.int32)
    row_mask = (tile_rows[:, None] == row_ids).astype(bf16)
    turned = jnp.transpose(tiles, (2, 0, 1))
    wide = turned[:, :, None, :] * row_mask[None, :, :, None]
    wide = wide.reshape(edge * slots, RB_DEV * edge)

    def forward(kept_operand):
        sent = jnp.dot(picks, kept_operand, preferred_element_type=f32).astype(bf16)
        fetched = spread(sent.reshape(owners, slots, width), "blk").reshape(edge * slots, width)
        return lax.dot_general(
            wide, fetched, (((0,), (0,)), ((), ())), preferred_element_type=f32
        ).astype(bf16)

    scaled = (kept_scale * kept_rows.astype(f32)).astype(bf16)
    range_rows = forward(scaled)
    terms = jnp.dot(wide, range_rows, preferred_element_type=f32).astype(bf16)
    arrived = spread(terms.reshape(owners, slots, width), "blk").reshape(owners * slots, width)
    back = lax.dot_general(picks, arrived, (((0,), (0,)), ((), ())), preferred_element_type=f32)
    weighted = ((kept_scale * kept_scale) * back).astype(bf16)
    power_rows = forward(weighted)

    side = lax.axis_index("col")
    other = lax.ppermute(power_rows, "col", [(0, 1), (1, 0)])
    left = jnp.where(side == 0, power_rows, other)
    right = jnp.where(side == 0, other, power_rows)
    all_rows = jnp.concatenate([left, right], axis=1)
    total_rows = all_rows.shape[0] * owners
    half = all_rows.shape[0] // cols
    gram_rows = lax.dynamic_slice_in_dim(all_rows, side * half, half, 0)
    partial = lax.dot_general(
        gram_rows, gram_rows, (((0,), (0,)), ((), ())), preferred_element_type=f32
    )
    everyone = ("blk", "col")
    parts = owners * cols
    share = spread(partial.reshape(parts, -1, edge), everyone).sum(0) / total_rows
    gram_matrix = spread(jnp.broadcast_to(share, (parts,) + share.shape), everyone)
    gram_matrix = gram_matrix.reshape(partial.shape)
    inverse = invert_factor(gram_matrix)
    own_inverse = lax.dynamic_slice_in_dim(inverse, side * width, width, 0)
    return jnp.dot(all_rows.astype(f32), own_inverse.T, precision=lax.Precision.HIGHEST)


def solution(mesh):
    placed = (P("blk", None, None), P("blk"), P("blk"), P("blk"), P("blk", "col"), P("blk"))
    return jax.shard_map(
        local, mesh=mesh, in_specs=placed, out_specs=P("blk", "col"), check_vma=False
    )
```

time: 1210 us -> 338 us (0.28)
  waiting for transfers between devices: 843 us -> 81.7 us
  other arithmetic: 170 us -> 5.28 us
  blocking collectives: 19.8 us -> 160 us
  starting transfers between devices: 77.6 us -> 17 us
  Pallas kernels: 0 us -> 49.7 us
  local copies, waits for them, and re-layouts: 51.7 us -> 4.34 us
  between operations: 17.4 us -> 0.8 us
    all_to_all x4 -> x2, waiting for transfers between devices: 568 us -> 75.3 us  [spread(): return lax.all_to_all(rows, axes, split_axis=0, concat_axis=0, tiled=True)]
    psum x1 -> x0, waiting for transfers between devices: 275 us -> none  [local(): gram_matrix = lax.psum(gram_of(tall_rows), ('blk', 'col')) / total_rows]
    all_to_all x2 -> x4, blocking collectives: 19.8 us -> 160 us  [spread(): return lax.all_to_all(rows, axes, split_axis=0, concat_axis=0, tiled=True)]
    another operation x18 -> x0, other arithmetic: 124 us -> none  [the longest x14 83.2 us: invert_factor(): lower_factor = jnp.linalg.cholesky(gram_matrix)]
    all_to_all x4 -> x2, starting transfers between devices: 77.6 us -> 14.2 us  [spread(): return lax.all_to_all(rows, axes, split_axis=0, concat_axis=0, tiled=True)]
    pallas_call x0 -> x1, Pallas kernels: none -> 49.7 us  [invert_factor(): pl.pallas_call(factor_body, out_shape=jax.ShapeDtypeStruct((n, n), jnp.fl...]
    gather x8 -> x0, local copies, waits for them, and re-layouts: 29.4 us -> none  [the longest x4 15.8 us: forward_step(): selected = jnp.take(fetched, col_group // own_blocks, axis=0)]
    select_n x10 -> x1, other arithmetic: 16 us -> 0.04 us  [local(): left = jnp.where(side == 0, power_rows, other)]
  transfers between devices with their start and end apart: 5 -> 3, of which waited for: 5 -> 3; matrix products, arithmetic and copies ran while one was open for 0% -> 1% of each run, Pallas kernels for 0% -> 0%
where the time goes in v1:
time: 338 us
  blocking collectives  160 us (47%)
  waiting for transfers between devices  81.7 us (24%)
  Pallas kernels  49.7 us (15%)
  matrix products  19.1 us (6%)
  starting transfers between devices  17 us (5%)
  other arithmetic  5.28 us (2%)
  local copies, waits for them, and re-layouts  4.34 us (1%)
    all_to_all x4, blocking collectives, spread(): return lax.all_to_all(rows, axes, split_axis=0, concat_axis=0, tiled=True)  160 us
    all_to_all x2, waiting for transfers between devices, spread(): return lax.all_to_all(rows, axes, split_axis=0, concat_axis=0, tiled=True)  75.3 us
    pallas_call x1, Pallas kernels, invert_factor(): pl.pallas_call(factor_body, out_shape=jax.ShapeDtypeStruct((n, n), jnp.fl...  49.7 us
    all_to_all x2, starting transfers between devices, spread(): return lax.all_to_all(rows, axes, split_axis=0, concat_axis=0, tiled=True)  14.2 us
    dot_general x2, matrix products, forward(): sent = jnp.dot(picks, kept_operand, preferred_element_type=f32).astype(bf16)  9.18 us
  transfers between devices with their start and end apart: 3, of which 3 were waited for; matrix products, arithmetic and copies ran while one was open for 1% of the time, Pallas kernels for 0%

profile of v1, /device:TPU:1, one launch (start us, length us, event | category | flops | bytes accessed | tf_op | source)
XLA Modules:
  0.0 337.5 jit_solution(14935282569266356283)
XLA Ops:
  0.7 0.7 fusion.38
  1.4 0.8 pad_maximum_fusion.3
  2.2 0.1 copy.17
  2.3 0.1 copy.18
  2.4 1.2 copy.41
  3.6 0.3 pad_maximum_fusion.2
  3.8 33.7 %all_to_all.30 = bf16[128,5,256]{2,1,0:T(8,128)(2,1)S(1)} all-to-all(bf16[128,5,256]{2,1,0:T(8,128)(2,1)S(1)} %pad_maximum_fusion.2), channel_id=1, replica_groups=mesh['blk'=128,'col'=2] {'blk'}, dimensions={0} | all-to-all | bytes 655360 | tf_op jit(solution)/shard_map/all_to_all | solution.py:12
  37.6 0.1 slice_convert_fusion.1
  37.7 0.1 fusion.34
  37.9 0.1 reshape.91
  38.0 0.1 slice_convert_fusion
  38.1 0.2 reshape.100
  38.3 2.6 fusion.3
  41.0 6.6 %all-to-all-start.1 = ((bf16[128,24,256]{2,1,0:T(8,128)(2,1)}), bf16[128,24,256]{2,1,0:T(8,128)(2,1)}, u32[]{:S(2)}, u32[]{:S(2)}) async-start(bf16[128,24,256]{2,1,0:T(8,128)(2,1)} %bitcast.7), calls=%async_computation.1 | async-start | bytes 3145728 | tf_op jit(solution)/shard_map/all_to_all | solution.py:12
  47.6 1.3 copy.15
  48.9 2.8 broadcast_multiply_fusion
  51.7 35.6 %all-to-all-done.1 = bf16[128,24,256]{2,1,0:T(8,128)(2,1)} async-done(((bf16[128,24,256]{2,1,0:T(8,128)(2,1)}), bf16[128,24,256]{2,1,0:T(8,128)(2,1)}, u32[]{:S(2)}, u32[]{:S(2)}) %all-to-all-start.1) | async-done | bytes 1572896 | tf_op jit(solution)/shard_map/all_to_all | solution.py:12
  87.3 6.0 %convolution_convert_fusion = bf16[3072,256]{1,0:T(8,128)(2,1)} fusion(bf16[384,8,4,128]{3,2,1,0:T(4,128)(2,1)S(1)} %bitcast.46, bf16[3072,256]{1,0:T(8,128)(2,1)} %bitcast.8), kind=kOutput, calls=%fused_computation.7 | convolution fusion | flops 1611530240 | bytes 6291456 | tf_op jit(solution)/shard_map/dot_general | solution.py:109
  93.4 7.7 %all-to-all-start.2 = ((bf16[128,24,256]{2,1,0:T(8,128)(2,1)}), bf16[128,24,256]{2,1,0:T(8,128)(2,1)}, u32[]{:S(2)}, u32[]{:S(2)}) async-start(bf16[128,24,256]{2,1,0:T(8,128)(2,1)} %bitcast.48), calls=%async_computation.2 | async-start | bytes 3145728 | tf_op jit(solution)/shard_map/all_to_all | solution.py:12
  101.1 39.7 %all-to-all-done.2 = bf16[128,24,256]{2,1,0:T(8,128)(2,1)} async-done(((bf16[128,24,256]{2,1,0:T(8,128)(2,1)}), bf16[128,24,256]{2,1,0:T(8,128)(2,1)}, u32[]{:S(2)}, u32[]{:S(2)}) %all-to-all-start.2) | async-done | bytes 1572896 | tf_op jit(solution)/shard_map/all_to_all | solution.py:12
  140.7 6.5 %fusion.4 = bf16[3072,256]{1,0:T(8,128)(2,1)} fusion(s32[3072]{0:T(1024)S(1)} %eq.49, bf16[128,24,256]{2,1,0:T(8,128)(2,1)} %all-to-all-done.2, s32[128,24]{1,0:T(8,128)S(1)} %fusion.34, f32[512]{0:T(512)S(1)} %mul.68), kind=kOutput, calls=%fused_computation.6 | convolution fusion | flops 1614807040 | bytes 3172352 | tf_op jit(solution)/shard_map/dot_general | solution.py:101
  147.3 47.2 %all_to_all.31 = bf16[128,24,256]{2,1,0:T(8,128)(2,1)S(1)} all-to-all(bf16[128,24,256]{2,1,0:T(8,128)(2,1)} %bitcast.49), channel_id=1, replica_groups=mesh['blk'=128,'col'=2] {'blk'}, dimensions={0} | all-to-all | bytes 3145728 | tf_op jit(solution)/shard_map/all_to_all | solution.py:12
  194.5 1.0 fusion.22
  195.6 2.7 collective-permute-start
  198.3 6.3 %collective-permute-done = bf16[512,256]{0,1:T(8,128)(2,1)S(1)} collective-permute-done((bf16[512,256]{0,1:T(8,128)(2,1)S(1)}, bf16[512,256]{0,1:T(8,128)(2,1)S(1)}, u32[]{:S(2)}, u32[]{:S(2)}) %collective-permute-start) | collective-permute-done | bytes 262176 | tf_op jit(solution)/shard_map/ppermute | solution.py:116
  204.7 0.3 fusion.30
  205.1 40.6 %all_to_all.32 = f32[256,8,128]{2,1,0:T(8,128)S(1)} all-to-all(f32[256,8,128]{2,1,0:T(8,128)S(1)} %reshape.97), channel_id=1, replica_groups=mesh['blk'=128,'col'=2] {'blk','col'}, dimensions={0} | all-to-all | bytes 2097152 | tf_op jit(solution)/shard_map/all_to_all | solution.py:12
  245.7 0.3 reduce_sum.9
  246.1 38.1 %all_to_all.33 = f32[256,8,128]{2,1,0:T(8,128)S(1)} all-to-all(f32[256,8,128]{2,1,0:T(8,128)S(1)} %broadcast_in_dim.10), channel_id=1, replica_groups=mesh['blk'=128,'col'=2] {'blk','col'}, dimensions={0} | all-to-all | bytes 2097152 | tf_op jit(solution)/shard_map/all_to_all | solution.py:12
  284.1 1.1 reshape.98.gram_ref
  285.3 49.7 %shard_map.64 = f32[512,512]{1,0:T(8,128)} custom-call(f32[512,512]{1,0:T(8,128)} %reshape.98.gram_ref), custom_call_target="tpu_custom_call" | custom-call | tf_op jit(solution)/shard_map/pallas_call | solution.py:59
  335.0 2.6 fusion.27
  (15 shorter events, 0.5 us)
Async XLA Ops:
  41.0 6.6 %copy-start = (bf16[24,128,128]{2,1,0:T(8,128)(2,1)S(1)}, bf16[24,128,128]{2,1,0:T(8,128)(2,1)}, u32[]{:S(2)}) copy-start(bf16[24,128,128]{2,1,0:T(8,128)(2,1)} %param.6) | copy-start | bytes 2359300
  41.0 46.4 %all-to-all-start.1 = ((bf16[128,24,256]{2,1,0:T(8,128)(2,1)}), bf16[128,24,256]{2,1,0:T(8,128)(2,1)}, u32[]{:S(2)}, u32[]{:S(2)}) async-start(bf16[128,24,256]{2,1,0:T(8,128)(2,1)} %bitcast.7), calls=%async_computation.1 | async-start | bytes 3145728 | tf_op jit(solution)/shard_map/all_to_all | solution.py:12
  47.5 1.3 copy-start.1
  93.4 47.4 %all-to-all-start.2 = ((bf16[128,24,256]{2,1,0:T(8,128)(2,1)}), bf16[128,24,256]{2,1,0:T(8,128)(2,1)}, u32[]{:S(2)}, u32[]{:S(2)}) async-start(bf16[128,24,256]{2,1,0:T(8,128)(2,1)} %bitcast.48), calls=%async_computation.2 | async-start | bytes 3145728 | tf_op jit(solution)/shard_map/all_to_all | solution.py:12
  195.6 9.1 %collective-permute-start = (bf16[512,256]{0,1:T(8,128)(2,1)S(1)}, bf16[512,256]{0,1:T(8,128)(2,1)S(1)}, u32[]{:S(2)}, u32[]{:S(2)}) collective-permute-start(bf16[512,256]{0,1:T(8,128)(2,1)S(1)} %fusion.22), channel_id=1, source_target_pairs={{0,1},{1,0},{2,3},{3,2},{4,5},{5,4},{6,7},{7,6},{8,9},{9,8},{10,11... | collective-permute-start | bytes 786440 | tf_op jit(solution)/shard_map/ppermute | solution.py:116
